TPU v7x, 256 devices: a whole 4x4x8 slice. The times are simulated.
256 devices in a mesh: rows: 64 (over x, z, core), cols: 4 (over y).
Axes of the slice: x: 4, y: 4, z: 8, core: 2. Of those that a mesh axis runs over, the one named last changes fastest.
Arguments:
- column_lists: int32 [256, 13], replicated, may hold values from -1 to 255, as said below
- block_values: bfloat16 [256, 13, 128, 128], P('rows'), as said below
Outputs:
- purified: bfloat16 [256, 13, 128, 128], P('rows', None, None, 'cols')
Inputs may be any that keep to these rules, and one draw needn't show every extreme that they name: `column_lists`: slot (13 - 1) // 2 of row i holds i. Slot s of row i holds -1 or a row j, and then slot 12 - s of row j holds i. There is an ordering of the rows, taken cyclically, in which the row in slot s of row i stands s - (13 - 1) // 2 places after row i. With owners the aligned groups of 4 rows, the slots of one owner's rows hold at most 2 rows of any one other owner, and some pair of owners has exactly 2. Over the slots s of one owner's rows that hold rows of one other owner, the sum of 13 - |s - (13 - 1) // 2| is at most 16, and exactly 16 for some pair of owners. block_values[j, 12 - s] is the transpose of block_values[i, s] where slot s of row i holds j; blocks of empty slots are zero.
All inputs are finite; a program needn't handle non-finite values.
Results may differ from a plain program's by a relative error of at most 0.0039.
Values may be sent and summed in bfloat16 or wider, within the bound.
No kernel may reach another device: no remote copies, remote signals or barrier semaphores. Data moves between devices by JAX's collectives and lax.ppermute only.
A program may use at most 128 MiB of HBM per device.

v0:
```python
import jax
import jax.numpy as jnp
from jax import lax
from jax.sharding import PartitionSpec as P

CAP = 2


def body(column_lists, block_values):
    rows_here = block_values.shape[0]
    slot_count = block_values.shape[1]
    block_size = block_values.shape[2]
    middle = (slot_count - 1) // 2
    owners = lax.axis_size("rows")
    strip_width = block_size // lax.axis_size("cols")
    row_index = lax.axis_index("rows")
    column_part = lax.axis_index("cols")
    all_rows = column_lists.shape[0]
    present = column_lists >= 0
    target = jnp.maximum(column_lists, 0)
    owner_of = target // rows_here
    home_owner = (jnp.arange(all_rows, dtype=jnp.int32) // rows_here)[:, None]
    crossing = present & (owner_of != home_owner)
    dest_hot = (
        crossing[:, :, None] & (owner_of[:, :, None] == jnp.arange(owners, dtype=jnp.int32))
    ).astype(jnp.int32)
    first_row = row_index * rows_here
    own_present = lax.dynamic_slice_in_dim(present, first_row, rows_here, 0)
    my_cross = lax.dynamic_slice_in_dim(crossing, first_row, rows_here, 0)
    my_owner = lax.dynamic_slice_in_dim(owner_of, first_row, rows_here, 0)
    my_target = lax.dynamic_slice_in_dim(target, first_row, rows_here, 0)
    full_rows = jnp.where(
        own_present[:, :, None, None], block_values, jnp.zeros((), block_values.dtype)
    )
    own_strip = lax.dynamic_slice_in_dim(full_rows, column_part * strip_width, strip_width, 3)
    slot_ids = jnp.arange(slot_count, dtype=jnp.int32)
    running = jnp.cumsum(dest_hot.reshape(owners, rows_here * slot_count, owners), axis=1)
    running = running.reshape(all_rows, slot_count, owners)
    ranking = jnp.sum(running * dest_hot, axis=2) - 1
    my_rank = lax.dynamic_slice_in_dim(ranking, first_row, rows_here, 0)
    filler = jnp.zeros((1, slot_count - 1, block_size, strip_width), own_strip.dtype)
    local_stack = jnp.concatenate([own_strip[:, : slot_count - 1], own_strip[:, 1:], filler], 0)
    zero_entry = 2 * rows_here
    slot_of = jnp.where(my_cross, my_owner * CAP + my_rank, owners * CAP)
    stack_entry = (
        jnp.arange(rows_here, dtype=jnp.int32)[:, None]
        + jnp.where(slot_ids < middle, 0, rows_here)[None, :]
    )
    source = jnp.full((owners * CAP + 1,), zero_entry, jnp.int32)
    source = source.at[slot_of.reshape(-1)].set(stack_entry.reshape(-1))[: owners * CAP]
    outgoing = local_stack[source]
    back_rank = ranking[my_target, (slot_count - 1 - slot_ids)[None, :]]
    local_pick = (
        owners * CAP + my_target - first_row + jnp.where(slot_ids > middle, 0, rows_here)[None, :]
    )
    remote_pick = my_owner * CAP + back_rank
    empty_entry = owners * CAP + zero_entry
    table_pick = jnp.where(
        own_present & (my_owner == row_index),
        local_pick,
        jnp.where(own_present, remote_pick, empty_entry),
    )
    table_pick = table_pick.at[:, middle].set(empty_entry)
    arrived = lax.all_to_all(outgoing, "rows", split_axis=0, concat_axis=0, tiled=True)
    lookup = jnp.concatenate([arrived, local_stack], 0)
    picked = lookup[table_pick]
    by_slot = []
    for slot_index in range(slot_count):
        offset = slot_index - middle
        if offset == 0:
            by_slot.append(own_strip)
        elif offset > 0:
            by_slot.append(
                jnp.pad(
                    picked[:, slot_index, : slot_count - offset],
                    ((0, 0), (offset, 0), (0, 0), (0, 0)),
                )
            )
        else:
            by_slot.append(
                jnp.pad(
                    picked[:, slot_index, -offset - 1 :], ((0, 0), (0, -offset), (0, 0), (0, 0))
                )
            )
    windows = jnp.stack(by_slot, 1)
    square_sum = jnp.einsum(
        "iapq,iasqc->ispc", full_rows, windows, preferred_element_type=jnp.float32
    )
    square = jnp.where(own_present[:, :, None, None], square_sum, 0.0).astype(jnp.bfloat16)
    cube_sum = jnp.einsum(
        "iapq,iasqc->ispc",
        lax.all_gather(square, "cols", axis=3, tiled=True),
        windows,
        preferred_element_type=jnp.float32,
    )
    purified = jnp.where(
        own_present[:, :, None, None], 3.0 * square.astype(jnp.float32) - 2.0 * cube_sum, 0.0
    )
    return purified.astype(jnp.bfloat16)


def solution(mesh):
    in_specs = (P(), P("rows", None, None, None))
    out_specs = P("rows", None, None, "cols")
    return jax.shard_map(body, mesh=mesh, in_specs=in_specs, out_specs=out_specs, check_vma=False)
```

profile of v0, /device:TPU:1, one launch (start us, length us, event | category | flops | bytes accessed | tf_op | source)
XLA Modules:
  0.0 390.3 jit_solution(5772552660954711740)
XLA Ops:
  6.6 0.8 copy.54
  7.4 0.1 broadcast_maximum_fusion
  7.5 0.1 reshape.111
  7.6 0.1 eq.23
  7.7 0.1 copy.58
  7.7 0.1 compare_and_fusion
  7.9 0.1 and.45
  8.0 0.1 copy.57
  8.1 2.7 select_reduce_fusion
  10.8 0.1 copy.59
  10.9 0.1 sub.36
  11.0 1.0 gather_fusion.1
  12.0 0.1 reshape.114
  12.1 2.8 copy.55
  14.9 0.1 reshape.102
  15.0 0.1 reshape.129
  15.1 0.7 scatter_custom_fusion
  15.9 0.2 broadcast_select_fusion
  16.1 0.0 copy-start
  16.1 0.1 constant_dynamic-slice_fusion
  16.2 0.0 copy-start.1
  16.2 0.0 copy-start.3
  16.2 1.1 copy-done
  17.3 0.1 copy-done.1
  17.4 0.1 copy-done.3
  17.5 0.1 pad_maximum_fusion.1
  17.6 8.0 %gather_fusion = bf16[128,12,128,32]{2,3,1,0:T(8,128)(2,1)} fusion(bf16[9,12,128,32]{2,3,1,0:T(8,128)(2,1)S(1)} %pad_maximum_fusion.1, s32[1024]{0:T(1024)S(1)} %pad_clamp_fusion.1), kind=kCustom, calls=%fused_computation | custom fusion | bytes 25166336 | tf_op jit(solution)/shard_map/gather | solution.py:51
  25.7 0.0 copy-start.2
  25.7 0.0 copy-start.4
  25.7 13.3 %all-to-all-start = ((bf16[128,12,128,32]{2,3,1,0:T(8,128)(2,1)}), bf16[128,12,128,32]{2,3,1,0:T(8,128)(2,1)}, u32[]{:S(2)}, u32[]{:S(2)}) async-start(bf16[128,12,128,32]{2,3,1,0:T(8,128)(2,1)} %gather_fusion), calls=%async_computation | async-start | bytes 25165824 | tf_op jit(solution)/shard_map/all_to_all | solution.py:64
  38.9 0.0 all-gather.2.cloned.1.call-start
  39.0 0.7 compare_reduce_fusion
  39.7 0.8 slice_select_fusion
  40.5 0.2 scatter.13
  40.7 0.1 reshape.119
  40.8 273.8 %all-to-all-done = bf16[128,12,128,32]{2,3,1,0:T(8,128)(2,1)} async-done(((bf16[128,12,128,32]{2,3,1,0:T(8,128)(2,1)}), bf16[128,12,128,32]{2,3,1,0:T(8,128)(2,1)}, u32[]{:S(2)}, u32[]{:S(2)}) %all-to-all-start) | async-done | bytes 12582944 | tf_op jit(solution)/shard_map/all_to_all | solution.py:64
  314.6 0.0 copy-done.2
  314.6 0.0 copy-done.4
  314.6 14.4 %pad_maximum_fusion = bf16[137,12,128,32]{2,3,1,0:T(8,128)(2,1)} fusion(bf16[1,12,128,32]{2,3,1,0:T(8,128)(2,1)S(1)} %broadcast_in_dim.85, bf16[4,12,128,32]{2,3,1,0:T(8,128)(2,1)S(1)} %copy-done.4, bf16[4,12,128,32]{2,3,1,0:T(8,128)(2,1)S(1)} %copy-done.2, bf16[128,12,128,32]{2,3,1,0:T(8,128)(2,1)} %all-to-all-done), kind=kLoop, calls=%fused_computation.4 | loop fusion | flops 20201472 | bytes 26935296 | tf_op jit(solution)/shard_map/concatenate | solution.py:65
  329.0 8.4 %gather_fusion.2 = bf16[52,12,128,32]{2,3,1,0:T(8,128)(2,1)} fusion(bf16[137,12,128,32]{2,3,1,0:T(8,128)(2,1)} %pad_maximum_fusion, s32[1024]{0:T(1024)S(1)} %pad_clamp_fusion), kind=kCustom, calls=%fused_computation.2 | custom fusion | bytes 10223824 | tf_op jit(solution)/shard_map/gather | solution.py:66
  337.4 1.1 slice_bitcast_fusion.10
  338.4 1.1 slice_bitcast_fusion.8
  339.5 1.1 slice_bitcast_fusion.6
  340.6 1.1 slice_bitcast_fusion.4
  341.7 1.1 slice_bitcast_fusion.2
  342.9 1.2 slice_bitcast_fusion
  344.1 0.1 bitcast_dynamic-update-slice_fusion.11
  344.2 0.1 bitcast_dynamic-update-slice_fusion.10
  344.3 0.1 bitcast_dynamic-update-slice_fusion.9
  344.4 0.1 bitcast_dynamic-update-slice_fusion.8
  344.4 0.1 bitcast_dynamic-update-slice_fusion.7
  344.5 1.1 bitcast_dynamic-update-slice_fusion.6
  345.6 0.1 bitcast_dynamic-update-slice_fusion.5
  345.7 0.1 bitcast_dynamic-update-slice_fusion.4
  345.7 0.1 bitcast_dynamic-update-slice_fusion.3
  345.8 0.1 bitcast_dynamic-update-slice_fusion.2
  345.9 0.1 bitcast_dynamic-update-slice_fusion.1
  346.0 0.1 bitcast_dynamic-update-slice_fusion
  346.1 0.0 copy-start.5
  346.1 2.4 copy-done.5
  348.5 2.4 fusion.35
  350.9 0.0 all-gather.2.cloned.1.call-update
  350.9 27.1 %all-gather.2.cloned.1.call-done = bf16[4,13,128,128]{2,3,1,0:T(8,128)(2,1)} async-done(((bf16[4,13,128,32]{2,3,1,0:T(8,128)(2,1)}), bf16[4,13,128,128]{2,3,1,0:T(8,128)(2,1)}) %all-gather.2.cloned.1.call-update) | async-done | bytes 1703952 | tf_op jit(solution)/shard_map/all_gather | solution.py:92
  378.0 5.4 %fusion.26 = bf16[4,13,128,32]{2,3,1,0:T(8,128)(2,1)} fusion(bf16[4,13,13,128,32]{3,4,1,2,0:T(8,128)(2,1)} %copy-done.5, bf16[4,13,128,128]{2,3,1,0:T(8,128)(2,1)} %all-gather.2.cloned.1.call-done, bf16[4,13,128,32]{2,3,1,0:T(8,128)(2,1)} %fusion.35, pred[4,13]{1,0:T(4,128)(4,1)S(1)} %get-tuple-element.18), kind=kOutput, calls=%fused_computation.21 | convolution fusion | flops 710115328 | bytes 8093748 | tf_op jit(solution)/shard_map/iapq,iasqc->ispc/dot_general | solution.py:90
  (14 shorter events, 0.1 us)
Async XLA Ops:
  16.1 1.2 copy-start
  16.2 1.2 copy-start.1
  16.2 1.3 copy-start.3
  25.7 288.9 %copy-start.2 = (bf16[4,12,128,32]{2,3,1,0:T(8,128)(2,1)S(1)}, bf16[4,12,128,32]{2,3,1,0:T(8,128)(2,1)}, u32[]{:S(2)}) copy-start(bf16[4,12,128,32]{2,3,1,0:T(8,128)(2,1)} %copy-done.1) | copy-start | bytes 1179652
  25.7 288.9 %copy-start.4 = (bf16[4,12,128,32]{2,3,1,0:T(8,128)(2,1)S(1)}, bf16[4,12,128,32]{2,3,1,0:T(8,128)(2,1)}, u32[]{:S(2)}) copy-start(bf16[4,12,128,32]{2,3,1,0:T(8,128)(2,1)} %copy-done.3) | copy-start | bytes 1179652
  25.7 288.9 %all-to-all-start = ((bf16[128,12,128,32]{2,3,1,0:T(8,128)(2,1)}), bf16[128,12,128,32]{2,3,1,0:T(8,128)(2,1)}, u32[]{:S(2)}, u32[]{:S(2)}) async-start(bf16[128,12,128,32]{2,3,1,0:T(8,128)(2,1)} %gather_fusion), calls=%async_computation | async-start | bytes 25165824 | tf_op jit(solution)/shard_map/all_to_all | solution.py:64
  38.9 339.1 %all-gather.2.cloned.1.call-start = ((), (), s32[]{:S(2)}) async-start(), calls=%async_computation.1 | async-start | bytes 2129920 | tf_op jit(solution)/shard_map/all_gather | solution.py:92
  346.1 2.4 copy-start.5
Sparse Core Ops, SparseCore 0:
  351.0 26.9 all-gather.1
where the time goes:
time: 391 us; the launch traced here: 390 us
  waiting for transfers between devices  301 us (77%)
  local copies, waits for them, and re-layouts  35.4 us (9%)
  other arithmetic  19.1 us (5%)
  between operations  13.7 us (4%)
  starting transfers between devices  13.3 us (3%)
  matrix products  7.86 us (2%)
    all_to_all x1, waiting for transfers between devices, body(): lax.all_to_all(outgoing, 'rows', split_axis=0, concat_axis=0, tiled=True)  274 us
    all_gather x1, waiting for transfers between devices, body(): lax.all_gather(square, 'cols', axis=3, tiled=True)  27.1 us
    concatenate x1, other arithmetic, body(): lookup = jnp.concatenate([arrived, local_stack], 0)  14.4 us
    all_to_all x1, starting transfers between devices, body(): lax.all_to_all(outgoing, 'rows', split_axis=0, concat_axis=0, tiled=True)  13.3 us
    unnamed x26, local copies, waits for them, and re-layouts  9.2 us
    gather x1, local copies, waits for them, and re-layouts, body(): picked = lookup[table_pick]  8.37 us
    gather x1, local copies, waits for them, and re-layouts, body(): outgoing = local_stack[source]  8.05 us
  transfers between devices with their start and end apart: 2, of which 2 were waited for; matrix products, arithmetic and copies ran while one was open for 0% of the time, Pallas kernels for 0%

commit v1 on v0

--- a/solution.py
+++ b/solution.py
@@ -4,6 +4,24 @@
 from jax.sharding import PartitionSpec as P
 
 CAP = 2
+
+
+def collect(shard, axis, dim):
+    ways, here, step = (lax.axis_size(axis), lax.axis_index(axis), shard.shape[dim])
+    shape = [n * ways if d == dim else n for d, n in enumerate(shard.shape)]
+    full = lax.dynamic_update_slice_in_dim(
+        jnp.zeros(shape, shard.dtype), shard, here * step, axis=dim
+    )
+    going_up = going_down = shard
+    for far in range(1, ways // 2 + 1):
+        going_up = lax.ppermute(going_up, axis, [(d, (d + 1) % ways) for d in range(ways)])
+        full = lax.dynamic_update_slice_in_dim(full, going_up, (here - far) % ways * step, axis=dim)
+        if 2 * far < ways:
+            going_down = lax.ppermute(going_down, axis, [(d, (d - 1) % ways) for d in range(ways)])
+            full = lax.dynamic_update_slice_in_dim(
+                full, going_down, (here + far) % ways * step, axis=dim
+            )
+    return full
 
 
 def body(column_lists, block_values):
@@ -88,10 +106,7 @@
     )
     square = jnp.where(own_present[:, :, None, None], square_sum, 0.0).astype(jnp.bfloat16)
     cube_sum = jnp.einsum(
-        "iapq,iasqc->ispc",
-        lax.all_gather(square, "cols", axis=3, tiled=True),
-        windows,
-        preferred_element_type=jnp.float32,
+        "iapq,iasqc->ispc", collect(square, "cols", 3), windows, preferred_element_type=jnp.float32
     )
     purified = jnp.where(
         own_present[:, :, None, None], 3.0 * square.astype(jnp.float32) - 2.0 * cube_sum, 0.0

time: 391 us -> 374 us (0.957)
  between operations: 13.7 us -> 0.37 us
  waiting for transfers between devices: 301 us -> 297 us
    all_gather x1 -> x0, waiting for transfers between devices: 27.1 us -> none  [body(): lax.all_gather(square, 'cols', axis=3, tiled=True)]
    ppermute x0 -> x3, waiting for transfers between devices: none -> 22.6 us  [the longest x2 22.6 us: collect(): lax.ppermute(going_up, axis, [(d, (d + 1) % ways) for d in range(ways)])]
  transfers between devices with their start and end apart: 2 -> 4, of which waited for: 2 -> 3; matrix products, arithmetic and copies ran while one was open for 0% -> 0% of each run, Pallas kernels for 0% -> 0%
where the time goes in v1:
time: 374 us; the launch traced here: 373 us
  waiting for transfers between devices  297 us (79%)
  local copies, waits for them, and re-layouts  33.5 us (9%)
  other arithmetic  19.1 us (5%)
  starting transfers between devices  16 us (4%)
  matrix products  7.58 us (2%)
    all_to_all x1, waiting for transfers between devices, body(): lax.all_to_all(outgoing, 'rows', split_axis=0, concat_axis=0, tiled=True)  274 us
    ppermute x2, waiting for transfers between devices, collect(): lax.ppermute(going_up, axis, [(d, (d + 1) % ways) for d in range(ways)])  22.6 us
    concatenate x1, other arithmetic, body(): lookup = jnp.concatenate([arrived, local_stack], 0)  14.4 us
    all_to_all x1, starting transfers between devices, body(): lax.all_to_all(outgoing, 'rows', split_axis=0, concat_axis=0, tiled=True)  13.3 us
    gather x1, local copies, waits for them, and re-layouts, body(): picked = lookup[table_pick]  8.38 us
    gather x1, local copies, waits for them, and re-layouts, body(): outgoing = local_stack[source]  8.04 us
  transfers between devices with their start and end apart: 4, of which 3 were waited for; matrix products, arithmetic and copies ran while one was open for 0% of the time, Pallas kernels for 0%

profile of v1, /device:TPU:1, one launch (start us, length us, event | category | flops | bytes accessed | tf_op | source)
XLA Modules:
  0.0 373.1 jit_solution(13799417877230735728)
XLA Ops:
  0.0 0.8 copy.63
  0.9 0.1 broadcast_maximum_fusion
  1.0 0.1 reshape.111
  1.0 0.1 eq.27
  1.1 0.1 copy.67
  1.2 0.1 compare_and_fusion
  1.3 0.1 and.58
  1.4 0.1 copy.66
  1.6 2.7 select_reduce_fusion
  4.3 0.1 copy.68
  4.4 0.1 sub.42
  4.5 1.0 gather_fusion.1
  5.4 0.1 reshape.114
  5.5 2.8 copy.64
  8.4 0.1 reshape.102
  8.5 0.1 reshape.129
  8.6 0.7 scatter_custom_fusion
  9.4 0.2 broadcast_select_fusion
  9.5 0.0 copy-start
  9.6 0.1 constant_dynamic-slice_fusion
  9.7 0.0 copy-start.3
  9.7 1.1 copy-done
  10.8 0.1 copy-done.1
  10.8 0.1 copy-done.3
  11.0 0.1 pad_maximum_fusion.1
  11.1 8.0 %gather_fusion = bf16[128,12,128,32]{2,3,1,0:T(8,128)(2,1)} fusion(bf16[9,12,128,32]{2,3,1,0:T(8,128)(2,1)S(1)} %pad_maximum_fusion.1, s32[1024]{0:T(1024)S(1)} %pad_clamp_fusion.1), kind=kCustom, calls=%fused_computation | custom fusion | bytes 25166336 | tf_op jit(solution)/shard_map/gather | solution.py:69
  19.1 13.3 %all-to-all-start = ((bf16[128,12,128,32]{2,3,1,0:T(8,128)(2,1)}), bf16[128,12,128,32]{2,3,1,0:T(8,128)(2,1)}, u32[]{:S(2)}, u32[]{:S(2)}) async-start(bf16[128,12,128,32]{2,3,1,0:T(8,128)(2,1)} %gather_fusion), calls=%async_computation | async-start | bytes 25165824 | tf_op jit(solution)/shard_map/all_to_all | solution.py:82
  32.4 0.7 compare_reduce_fusion
  33.1 0.7 slice_select_fusion
  33.8 0.2 scatter.13
  34.0 0.1 reshape.119
  34.1 274.0 %all-to-all-done = bf16[128,12,128,32]{2,3,1,0:T(8,128)(2,1)} async-done(((bf16[128,12,128,32]{2,3,1,0:T(8,128)(2,1)}), bf16[128,12,128,32]{2,3,1,0:T(8,128)(2,1)}, u32[]{:S(2)}, u32[]{:S(2)}) %all-to-all-start) | async-done | bytes 12582944 | tf_op jit(solution)/shard_map/all_to_all | solution.py:82
  308.1 14.4 %pad_maximum_fusion = bf16[137,12,128,32]{2,3,1,0:T(8,128)(2,1)} fusion(bf16[1,12,128,32]{2,3,1,0:T(8,128)(2,1)S(1)} %broadcast_in_dim.86, bf16[4,12,128,32]{2,3,1,0:T(8,128)(2,1)S(1)} %copy-done.4, bf16[4,12,128,32]{2,3,1,0:T(8,128)(2,1)S(1)} %copy-done.2, bf16[128,12,128,32]{2,3,1,0:T(8,128)(2,1)} %all-to-all-done), kind=kLoop, calls=%fused_computation.4 | loop fusion | flops 20201472 | bytes 26935296 | tf_op jit(solution)/shard_map/concatenate | solution.py:83
  322.5 8.4 %gather_fusion.2 = bf16[52,12,128,32]{2,3,1,0:T(8,128)(2,1)} fusion(bf16[137,12,128,32]{2,3,1,0:T(8,128)(2,1)} %pad_maximum_fusion, s32[1024]{0:T(1024)S(1)} %pad_clamp_fusion), kind=kCustom, calls=%fused_computation.2 | custom fusion | bytes 10223824 | tf_op jit(solution)/shard_map/gather | solution.py:84
  330.8 1.1 slice_bitcast_fusion.10
  331.9 1.1 slice_bitcast_fusion.8
  333.0 1.1 slice_bitcast_fusion.6
  334.1 1.1 slice_bitcast_fusion.4
  335.2 1.1 slice_bitcast_fusion.2
  336.4 1.2 slice_bitcast_fusion
  337.6 0.1 bitcast_dynamic-update-slice_fusion.11
  337.7 0.1 bitcast_dynamic-update-slice_fusion.10
  337.8 0.1 bitcast_dynamic-update-slice_fusion.9
  337.9 0.1 bitcast_dynamic-update-slice_fusion.8
  337.9 0.1 bitcast_dynamic-update-slice_fusion.7
  338.0 1.1 bitcast_dynamic-update-slice_fusion.6
  339.1 0.1 bitcast_dynamic-update-slice_fusion.5
  339.2 0.1 bitcast_dynamic-update-slice_fusion.4
  339.2 0.1 bitcast_dynamic-update-slice_fusion.3
  339.3 0.1 bitcast_dynamic-update-slice_fusion.2
  339.4 0.1 bitcast_dynamic-update-slice_fusion.1
  339.5 0.1 bitcast_dynamic-update-slice_fusion
  339.6 0.4 broadcast_in_dim.85
  340.0 2.6 constant_dynamic-update-slice_fusion.3
  342.6 1.3 collective-permute-start
  343.9 1.4 collective-permute-start.1
  345.3 10.5 %collective-permute-done = bf16[4,13,128,32]{2,3,1,0:T(8,128)(2,1)S(1)} collective-permute-done((bf16[4,13,128,32]{2,3,1,0:T(8,128)(2,1)}, bf16[4,13,128,32]{2,3,1,0:T(8,128)(2,1)S(1)}, u32[]{:S(2)}, u32[]{:S(2)}) %collective-permute-start) | collective-permute-done | bytes 426016 | tf_op jit(solution)/shard_map/ppermute | solution.py:17
  355.8 0.0 collective-permute-start.2
  355.8 0.1 constant_dynamic-update-slice_fusion.2
  355.9 0.0 collective-permute-done.1
  355.9 0.1 constant_dynamic-update-slice_fusion.1
  356.0 12.0 %collective-permute-done.2 = bf16[4,13,128,32]{2,3,1,0:T(8,128)(2,1)S(1)} collective-permute-done((bf16[4,13,128,32]{2,3,1,0:T(8,128)(2,1)S(1)}, bf16[4,13,128,32]{2,3,1,0:T(8,128)(2,1)S(1)}, u32[]{:S(2)}, u32[]{:S(2)}) %collective-permute-start.2) | collective-permute-done | bytes 426016 | tf_op jit(solution)/shard_map/ppermute | solution.py:17
  368.0 0.1 constant_dynamic-update-slice_fusion
  368.1 5.0 %fusion.26 = bf16[4,13,128,32]{2,3,1,0:T(8,128)(2,1)} fusion(bf16[4,13,13,128,32]{3,4,1,2,0:T(8,128)(2,1)} %copy-done.5, bf16[4,13,128,128]{2,3,1,0:T(8,128)(2,1)S(1)} %constant_dynamic-update-slice_fusion, bf16[4,13,128,32]{2,3,1,0:T(8,128)(2,1)} %get-tuple-element.39, pred[4,13]{1,0:T(4,128)(4,1)S(1)} %get-tuple-element.18), kind=kOutput, calls=%fused_computation.21 | convolution fusion | flops 710115328 | bytes 8093748 | tf_op jit(solution)/shard_map/iapq,iasqc->ispc/dot_general | solution.py:108
  (21 shorter events, 0.2 us)
Async XLA Ops:
  9.5 1.2 copy-start
  9.7 1.2 copy-start.1
  9.7 1.3 copy-start.3
  19.1 288.9 %copy-start.2 = (bf16[4,12,128,32]{2,3,1,0:T(8,128)(2,1)S(1)}, bf16[4,12,128,32]{2,3,1,0:T(8,128)(2,1)}, u32[]{:S(2)}) copy-start(bf16[4,12,128,32]{2,3,1,0:T(8,128)(2,1)} %copy-done.1) | copy-start | bytes 1179652
  19.1 288.9 %copy-start.4 = (bf16[4,12,128,32]{2,3,1,0:T(8,128)(2,1)S(1)}, bf16[4,12,128,32]{2,3,1,0:T(8,128)(2,1)}, u32[]{:S(2)}) copy-start(bf16[4,12,128,32]{2,3,1,0:T(8,128)(2,1)} %copy-done.3) | copy-start | bytes 1179652
  19.1 288.9 %all-to-all-start = ((bf16[128,12,128,32]{2,3,1,0:T(8,128)(2,1)}), bf16[128,12,128,32]{2,3,1,0:T(8,128)(2,1)}, u32[]{:S(2)}, u32[]{:S(2)}) async-start(bf16[128,12,128,32]{2,3,1,0:T(8,128)(2,1)} %gather_fusion), calls=%async_computation | async-start | bytes 25165824 | tf_op jit(solution)/shard_map/all_to_all | solution.py:82
  339.6 3.0 copy-start.5
  342.6 13.3 %collective-permute-start = (bf16[4,13,128,32]{2,3,1,0:T(8,128)(2,1)}, bf16[4,13,128,32]{2,3,1,0:T(8,128)(2,1)S(1)}, u32[]{:S(2)}, u32[]{:S(2)}) collective-permute-start(bf16[4,13,128,32]{2,3,1,0:T(8,128)(2,1)} %get-tuple-element.39), channel_id=1, source_target_pairs={{0,1},{1,2},{2,3},{3,0},{4,5},{5,6},{6,7},{7,4},{8,9},{9,10},{10,1... | collective-permute-start | bytes 1277960 | tf_op jit(solution)/shard_map/ppermute | solution.py:17
  343.9 12.1 %collective-permute-start.1 = (bf16[4,13,128,32]{2,3,1,0:T(8,128)(2,1)}, bf16[4,13,128,32]{2,3,1,0:T(8,128)(2,1)S(1)}, u32[]{:S(2)}, u32[]{:S(2)}) collective-permute-start(bf16[4,13,128,32]{2,3,1,0:T(8,128)(2,1)} %get-tuple-element.39), channel_id=1, source_target_pairs={{0,3},{1,0},{2,1},{3,2},{4,7},{5,4},{6,5},{7,6},{8,11},{9,8},{10,9... | collective-permute-start | bytes 1277960 | tf_op jit(solution)/shard_map/ppermute | solution.py:20
  355.8 12.2 %collective-permute-start.2 = (bf16[4,13,128,32]{2,3,1,0:T(8,128)(2,1)S(1)}, bf16[4,13,128,32]{2,3,1,0:T(8,128)(2,1)S(1)}, u32[]{:S(2)}, u32[]{:S(2)}) collective-permute-start(bf16[4,13,128,32]{2,3,1,0:T(8,128)(2,1)S(1)} %collective-permute-done), channel_id=1, source_target_pairs={{0,1},{1,2},{2,3},{3,0},{4,5},{5,6},{6,7},{7,4},{8,9},{9,10},{10,1... | collective-permute-start | bytes 1277960 | tf_op jit(solution)/shard_map/ppermute | solution.py:17
